TPU v7x, 32 devices: a whole 2x2x4 slice. The times are simulated.
32 devices in a mesh: section: 4 (over y, core), space: 8 (over z, x).
Axes of the slice: x: 2, y: 2, z: 4, core: 2. Of those that a mesh axis runs over, the one named last changes fastest.
Arguments:
- features: bfloat16 [4, 2048, 256], P('section', 'space'), may hold values from -6 to 6
- out_grad: bfloat16 [4, 2048, 256], P('section', 'space'), may hold values from -6 to 6
- weight: bfloat16 [4, 27, 256, 256], P('section'), may hold values from -0.078125 to 0.078125
- counts: int32 [4, 16], P('section', 'space'), may hold values from 16 to 128
- local_rows: int32 [4, 27, 2048], P('section', None, 'space'), may hold values from -1 to 255, as said below
- send_rows: int32 [4, 8, 27, 8, 2], P('section', 'space'), may hold values from -1 to 255, as said below
- recv_rows: int32 [4, 8, 27, 8, 2], P('section', 'space'), may hold values from -1 to 255, as said below
Outputs:
- handoff: bfloat16 [4, 2048, 256], P('section', 'space')
- weight_grad: float32 [4, 6912, 256], P('section', 'space')
Inputs may be any that keep to these rules, and one draw needn't show every extreme that they name: `local_rows`: -1 where a voxel has no pair on its own device at that offset. `send_rows`: for each offset and two different devices, the first 1 to 2 slots are used and the rest are -1; a device's slots to itself are all -1; for every sending device there is one offset at which all 2 slots to every other device are used. `recv_rows`: slot for slot the pairs of send_rows seen from the receiving device, -1 in the same empty slots.
All inputs are finite; a program needn't handle non-finite values.
Results may differ from a plain program's by a relative error of at most 0.0019.
Values may be sent and summed in bfloat16 or wider, within the bound.
No kernel may reach another device: no remote copies, remote signals or barrier semaphores. Data moves between devices by JAX's collectives and lax.ppermute only.
A program may use at most 64 MiB of HBM per device.

v0:
```python
import jax
import jax.numpy as jnp
from jax import lax
from jax.sharding import PartitionSpec as P

BLOCK = 128


def from_behind(block, axis, distance):
    devices = range(lax.axis_size(axis))
    route = [(i - distance, i) for i in devices if i - distance in devices]
    return lax.ppermute(block, axis, route)


def take_rows(source, row_index, nothing):
    picked = jnp.take(source, jnp.maximum(row_index, 0), axis=0)
    return jnp.where((row_index >= 0)[..., None], picked, nothing)


def body(features, out_grad, weight, counts, local_rows, send_rows, recv_rows):
    inputs = features[0]
    gradient = out_grad[0]
    kernel = weight[0]
    rows_dev = inputs.shape[0]
    channels = inputs.shape[1]
    offsets = kernel.shape[0]
    inside = (jnp.arange(BLOCK, dtype=jnp.int32)[None, :] < counts[0][:, None]).reshape(rows_dev, 1)
    nothing = jnp.zeros((), inputs.dtype)
    xmask = jnp.where(inside, inputs, nothing)
    gmask = jnp.where(inside, gradient, nothing)
    local_map = local_rows[0].T
    gathered = take_rows(gmask, local_map, nothing)
    input_grad = lax.dot_general(
        gathered, kernel, (((1, 2), (0, 1)), ((), ())), preferred_element_type=jnp.float32
    )
    weight_grad = lax.dot_general(
        gathered, xmask, (((0,), (0,)), ((), ())), preferred_element_type=jnp.float32
    )
    send_map = send_rows[0, 0]
    recv_map = recv_rows[0, 0]
    flat_shape = (offsets, -1, channels)
    outgoing = take_rows(gmask, send_map, nothing)
    partial_value = (
        lax.dot_general(
            outgoing.reshape(flat_shape),
            kernel,
            (((2,), (1,)), ((0,), (0,))),
            preferred_element_type=jnp.float32,
        )
        .astype(jnp.bfloat16)
        .reshape(outgoing.shape)
    )
    arrived = lax.all_to_all(partial_value, "space", split_axis=1, concat_axis=1, tiled=True)
    returned = lax.all_to_all(
        take_rows(xmask, recv_map, nothing), "space", split_axis=1, concat_axis=1, tiled=True
    )
    weight_grad = weight_grad + lax.dot_general(
        outgoing.reshape(flat_shape),
        returned.reshape(flat_shape),
        (((1,), (1,)), ((0,), (0,))),
        preferred_element_type=jnp.float32,
    )
    incoming = arrived.reshape(-1, channels).astype(jnp.float32)
    target = jnp.where(recv_map >= 0, recv_map, rows_dev).reshape(-1)
    input_grad = input_grad.at[target].add(incoming, mode="drop")
    result = jnp.where(inside, input_grad, 0.0).astype(jnp.bfloat16)
    handoff = from_behind(result, "section", -1)
    loss_scale = float(rows_dev * lax.axis_size("space")) ** (-0.5)
    summed = lax.psum_scatter(
        (weight_grad * loss_scale).reshape(offsets * channels, channels),
        "space",
        scatter_dimension=0,
        tiled=True,
    )
    return (handoff[None], summed[None])


def solution(mesh):
    placed = (
        P("section", "space", None),
        P("section", "space", None),
        P("section", None, None, None),
        P("section", "space"),
        P("section", None, "space"),
        P("section", "space", None, None, None),
        P("section", "space", None, None, None),
    )
    return jax.shard_map(
        body,
        mesh=mesh,
        in_specs=placed,
        out_specs=(P("section", "space", None), P("section", "space", None)),
        check_vma=False,
    )
```

profile of v0, /device:TPU:0, one launch (start us, length us, event | category | flops | bytes accessed | tf_op | source)
XLA Modules:
  0.0 275.7 jit_solution(11968080390307770625)
XLA Ops:
  15.3 3.1 %gather_fusion.1 = bf16[432,256]{1,0:T(8,128)(2,1)} fusion(bf16[256,256]{1,0:T(8,128)(2,1)} %bitcast_select_fusion.1, s32[1024]{0:T(1024)S(1)} %pad_clamp_fusion.2), kind=kCustom, calls=%fused_computation.clone | custom fusion | bytes 444096 | tf_op jit(solution)/shard_map/jit(_take)/gather | solution.py:16
  18.4 1.7 reshape.145
  20.1 2.3 broadcast_select_fusion.3
  25.0 2.2 fusion.4
  27.2 1.7 reshape.100
  28.9 1.8 copy.90
  30.7 7.3 %all-to-all-start = ((bf16[27,8,2,256]{3,2,0,1:T(2,128)(2,1)}), bf16[27,8,2,256]{3,2,0,1:T(2,128)(2,1)}, u32[]{:S(2)}, u32[]{:S(2)}) async-start(bf16[27,8,2,256]{3,2,0,1:T(2,128)(2,1)} %copy.90), calls=%async_computation | async-start | bytes 442368 | tf_op jit(solution)/shard_map/all_to_all | solution.py:53
  48.8 1.7 reshape.122
  55.4 18.5 %gather_fusion = bf16[6912,256]{1,0:T(8,128)(2,1)} fusion(bf16[256,256]{1,0:T(8,128)(2,1)} %bitcast_select_fusion.1, s32[7168]{0:T(1024)} %pad_clamp_fusion), kind=kCustom, calls=%fused_computation.2 | custom fusion | bytes 7105536 | tf_op jit(solution)/shard_map/jit(_take)/gather | solution.py:16
  73.9 6.4 %reshape.121 = bf16[256,27,256]{2,1,0:T(8,128)(2,1)} reshape(bf16[6912,256]{1,0:T(8,128)(2,1)} %gather_fusion) | data formatting | bytes 7077888 | tf_op jit(solution)/shard_map/jit(_take)/gather | solution.py:16
  80.3 7.6 %select_select_fusion = bf16[256,27,256]{2,1,0:T(8,128)(2,1)} fusion(bf16[256,27,256]{2,1,0:T(8,128)(2,1)} %reshape.121, pred[256,27]{1,0:T(8,128)(4,1)} %copy.81, pred[256,27]{1,0:T(8,128)(4,1)} %bitcast.53), kind=kLoop, calls=%fused_computation.5 | loop fusion | flops 3538944 | bytes 7091712 | tf_op jit(solution)/shard_map/jit(_where)/select_n | solution.py:17
  87.9 7.4 %copy.93 = bf16[256,27,256]{0,2,1:T(8,128)(2,1)} copy(bf16[256,27,256]{2,1,0:T(8,128)(2,1)} %select_select_fusion) | data formatting | bytes 7077888 | tf_op jit(solution)/shard_map/jit(_where)/select_n | solution.py:17
  95.3 3.8 %fusion.7 = f32[256,256]{1,0:T(8,128)} fusion(bf16[256,27,256]{0,2,1:T(8,128)(2,1)} %copy.93, bf16[1,27,256,256]{3,2,1,0:T(8,128)(2,1)S(1)} %copy-done), kind=kOutput, calls=%fused_computation.11 | convolution fusion | flops 905969664 | bytes 7340032 | tf_op jit(solution)/shard_map/dot_general | solution.py:33
  101.1 2.1 reshape.132
  103.1 4.7 %scatter_fusion = f32[256,256]{1,0:T(8,128)} fusion(f32[256,256]{1,0:T(8,128)} %fusion.7, s32[432]{0:T(512)S(1)} %bitcast.54, f32[432,256]{1,0:T(8,128)} %reshape.132), kind=kCustom, calls=%fused_computation.3 | custom fusion | flops 110592 | bytes 1328832 | tf_op jit(solution)/shard_map/scatter-add | solution.py:65
  107.9 1.8 bitcast_select_fusion
  109.7 3.1 %gather_fusion.2 = bf16[432,256]{1,0:T(8,128)(2,1)} fusion(bf16[256,256]{1,0:T(8,128)(2,1)} %get-tuple-element.7, s32[1024]{0:T(1024)S(1)} %pad_clamp_fusion.1), kind=kCustom, calls=%fused_computation.1.clone | custom fusion | bytes 444096 | tf_op jit(solution)/shard_map/jit(_take)/gather | solution.py:16
  112.8 1.7 reshape.149
  114.5 2.3 broadcast_select_fusion.2
  116.8 13.7 %all_to_all.10 = bf16[27,8,2,256]{3,2,0,1:T(2,128)(2,1)S(1)} all-to-all(bf16[27,8,2,256]{3,2,0,1:T(2,128)(2,1)S(1)} %broadcast_select_fusion.2), channel_id=1, replica_groups=mesh['section'=4,'space'=8] {'space'}, dimensions={1} | all-to-all | bytes 442368 | tf_op jit(solution)/shard_map/all_to_all | solution.py:54
  133.1 2.3 fusion.11
  135.4 4.0 %add_multiply_fusion = f32[27,256,256]{2,1,0:T(8,128)} fusion(f32[27,256,256]{2,1,0:T(8,128)S(1)} %fusion.11, bf16[256,27,256]{0,2,1:T(8,128)(2,1)S(1)} %copy-done.1, bf16[256,256]{1,0:T(8,128)(2,1)S(1)} %copy-done.2), kind=kOutput, calls=%fused_computation.4 | convolution fusion | flops 909508608 | bytes 17825792 | tf_op jit(solution)/shard_map/dot_general | solution.py:36
  140.7 2.3 collective-permute-done
  143.0 124.3 %reduce-scatter.2.cloned.1.call-done = f32[864,256]{1,0:T(8,128)} async-done(((f32[6912,256]{1,0:T(8,128)}), f32[864,256]{1,0:T(8,128)}) %reduce-scatter.2.cloned.1.call-update) | async-done | bytes 884752 | tf_op jit(solution)/shard_map/reduce_scatter | solution.py:69
  (49 shorter events, 33.7 us)
Async XLA Ops:
  7.2 17.8 %copy-start = (bf16[1,27,256,256]{3,2,1,0:T(8,128)(2,1)S(1)}, bf16[1,27,256,256]{3,2,1,0:T(8,128)(2,1)}, u32[]{:S(2)}) copy-start(bf16[1,27,256,256]{3,2,1,0:T(8,128)(2,1)} %param.11) | copy-start | bytes 10616836
  18.4 19.6 %copy-start.4 = (s32[1,1,27,8,2]{2,4,3,1,0:T(2,128)S(1)}, s32[1,1,27,8,2]{2,4,3,1,0:T(2,128)}, u32[]{:S(2)}) copy-start(s32[1,1,27,8,2]{2,4,3,1,0:T(2,128)} %param.15) | copy-start | bytes 5188
  30.7 68.4 %all-to-all-start = ((bf16[27,8,2,256]{3,2,0,1:T(2,128)(2,1)}), bf16[27,8,2,256]{3,2,0,1:T(2,128)(2,1)}, u32[]{:S(2)}, u32[]{:S(2)}) async-start(bf16[27,8,2,256]{3,2,0,1:T(2,128)(2,1)} %copy.90), calls=%async_computation | async-start | bytes 442368 | tf_op jit(solution)/shard_map/all_to_all | solution.py:53
  38.0 229.4 %reduce-scatter.2.cloned.1.call-start = ((), (), s32[]{:S(2)}) async-start(), calls=%async_computation.3 | async-start | bytes 7962624 | tf_op jit(solution)/shard_map/reduce_scatter | solution.py:69
  40.0 1.4 copy-start.3
  103.1 4.7 %copy-start.5 = (pred[256]{0:T(512)(128)(4,1)S(1)}, pred[256]{0:T(512)(128)(4,1)}, u32[]{:S(2)}) copy-start(pred[256]{0:T(512)(128)(4,1)} %compare_bitcast_fusion.2) | copy-start | bytes 772
  133.1 2.3 copy-start.1
  133.1 2.3 copy-start.2
  139.4 3.6 %collective-permute-start = (bf16[256,256]{1,0:T(8,128)(2,1)}, bf16[256,256]{1,0:T(8,128)(2,1)}, u32[]{:S(2)}, u32[]{:S(2)}) collective-permute-start(bf16[256,256]{1,0:T(8,128)(2,1)} %get-tuple-element.8), channel_id=1, source_target_pairs={{8,0},{16,8},{24,16},{9,1},{17,9},{25,17},{10,2},{18,10},{26,18},{... | collective-permute-start | bytes 393224 | tf_op jit(solution)/shard_map/ppermute | solution.py:12
Sparse Core Ops, SparseCore 0:
  139.6 127.7 reduce-scatter.1
where the time goes:
time: 278 us; the launch traced here: 276 us
  waiting for transfers between devices  127 us (46%)
  local copies, waits for them, and re-layouts  71 us (26%)
  other arithmetic  29.3 us (11%)
  between operations  14.2 us (5%)
  blocking collectives  13.7 us (5%)
  matrix products  12.3 us (4%)
  starting transfers between devices  8.61 us (3%)
    reduce_scatter x1, waiting for transfers between devices, body(): lax.psum_scatter((weight_grad * loss_scale).reshape(offsets * channels, c...  124 us
    gather x6, local copies, waits for them, and re-layouts, take_rows(): picked = jnp.take(source, jnp.maximum(row_index, 0), axis=0)  34.5 us
    all_to_all x1, blocking collectives, body(): lax.all_to_all(take_rows(xmask, recv_map, nothing), 'space', split_axis=1...  13.7 us
    select_n x3, other arithmetic, take_rows(): return jnp.where((row_index >= 0)[..., None], picked, nothing)  12.3 us
    select_n x2, local copies, waits for them, and re-layouts, take_rows(): return jnp.where((row_index >= 0)[..., None], picked, nothing)  8.23 us
    all_to_all x1, starting transfers between devices, body(): lax.all_to_all(partial_value, 'space', split_axis=1, concat_axis=1, tiled...  7.28 us
  transfers between devices with their start and end apart: 3, of which 2 were waited for; matrix products, arithmetic and copies ran while one was open for 22% of the time, Pallas kernels for 0%

commit v1 on v0

--- a/solution.py
+++ b/solution.py
@@ -4,6 +4,30 @@
 from jax.sharding import PartitionSpec as P
 
 BLOCK = 128
+
+
+def split_up(shard, dim, devices):
+    lengths = shard.shape
+    pieces = shard.reshape(*lengths[:dim], devices, lengths[dim] // devices, *lengths[dim + 1 :])
+    return jnp.moveaxis(pieces, dim, 0)
+
+
+def joined_along(blocks, dim):
+    blocks = jnp.moveaxis(blocks, 0, dim)
+    shape = blocks.shape
+    return blocks.reshape(*shape[:dim], shape[dim] * shape[dim + 1], *shape[dim + 2 :])
+
+
+def rotated_exchange(array, axis, split_dim, concat_dim):
+    size, index = (lax.axis_size(axis), lax.axis_index(axis))
+    tiles = split_up(array, split_dim, size)
+    whole = tiles
+    for step in range(1, size):
+        target, source = ((index + step) % size, (index - step) % size)
+        sent = lax.dynamic_index_in_dim(tiles, target, 0)
+        other = lax.ppermute(sent, axis, [(i, (i + step) % size) for i in range(size)])
+        whole = lax.dynamic_update_slice_in_dim(whole, other, source, axis=0)
+    return joined_along(whole, concat_dim)
 
 
 def from_behind(block, axis, distance):
@@ -51,9 +75,7 @@
         .reshape(outgoing.shape)
     )
     arrived = lax.all_to_all(partial_value, "space", split_axis=1, concat_axis=1, tiled=True)
-    returned = lax.all_to_all(
-        take_rows(xmask, recv_map, nothing), "space", split_axis=1, concat_axis=1, tiled=True
-    )
+    returned = rotated_exchange(take_rows(xmask, recv_map, nothing), "space", 1, 1)
     weight_grad = weight_grad + lax.dot_general(
         outgoing.reshape(flat_shape),
         returned.reshape(flat_shape),

time: 278 us -> 291 us (1.047)
  blocking collectives: 13.7 us -> 0 us
  starting transfers between devices: 8.61 us -> 21.2 us
  matrix products: 12.3 us -> 19.3 us
  other arithmetic: 29.3 us -> 33.3 us
    all_to_all x1 -> x0, blocking collectives: 13.7 us -> none  [body(): lax.all_to_all(take_rows(xmask, recv_map, nothing), 'space', split_axis=1...]
    ppermute x0 -> x7, starting transfers between devices: none -> 12.6 us  [rotated_exchange(): lax.ppermute(sent, axis, [(i, (i + step) % size) for i in range(size)])]
    dot_general x1, matrix products: 2.31 us -> 7.26 us  [body(): lax.dot_general(outgoing.reshape(flat_shape), returned.reshape(flat_shape...]
    dynamic_update_slice x0 -> x7, local copies, waits for them, and re-layouts: none -> 4.4 us  [rotated_exchange(): whole = lax.dynamic_update_slice_in_dim(whole, other, source, axis=0)]
    select_n x2 -> x1, local copies, waits for them, and re-layouts: 8.23 us -> 7.41 us  [take_rows(): return jnp.where((row_index >= 0)[..., None], picked, nothing)]
  transfers between devices with their start and end apart: 3 -> 10, of which waited for: 2 -> 2; matrix products, arithmetic and copies ran while one was open for 22% -> 24% of each run, Pallas kernels for 0% -> 0%
where the time goes in v1:
time: 291 us; the launch traced here: 289 us
  waiting for transfers between devices  128 us (44%)
  local copies, waits for them, and re-layouts  73.1 us (25%)
  other arithmetic  33.3 us (11%)
  starting transfers between devices  21.2 us (7%)
  matrix products  19.3 us (7%)
  between operations  14.1 us (5%)
    reduce_scatter x1, waiting for transfers between devices, body(): lax.psum_scatter((weight_grad * loss_scale).reshape(offsets * channels, c...  126 us
    gather x6, local copies, waits for them, and re-layouts, take_rows(): picked = jnp.take(source, jnp.maximum(row_index, 0), axis=0)  34.4 us
    ppermute x7, starting transfers between devices, rotated_exchange(): lax.ppermute(sent, axis, [(i, (i + step) % size) for i in range(size)])  12.6 us
    select_n x3, other arithmetic, take_rows(): return jnp.where((row_index >= 0)[..., None], picked, nothing)  11.5 us
    select_n x1, local copies, waits for them, and re-layouts, take_rows(): return jnp.where((row_index >= 0)[..., None], picked, nothing)  7.41 us
    all_to_all x1, starting transfers between devices, body(): lax.all_to_all(partial_value, 'space', split_axis=1, concat_axis=1, tiled...  7.28 us
    dot_general x1, matrix products, body(): lax.dot_general(outgoing.reshape(flat_shape), returned.reshape(flat_shape...  7.26 us
    dot_general x1, matrix products, body(): lax.dot_general(gathered, xmask, (((0,), (0,)), ((), ())), preferred_elem...  5.95 us
  transfers between devices with their start and end apart: 10, of which 2 were waited for; matrix products, arithmetic and copies ran while one was open for 24% of the time, Pallas kernels for 0%

profile of v1, /device:TPU:0, one launch (start us, length us, event | category | flops | bytes accessed | tf_op | source)
XLA Modules:
  0.0 289.2 jit_solution(18088367469687221452)
XLA Ops:
  14.5 3.1 %gather_fusion.1 = bf16[432,256]{1,0:T(8,128)(2,1)} fusion(bf16[256,256]{1,0:T(8,128)(2,1)} %bitcast_select_fusion.1, s32[1024]{0:T(1024)S(1)} %pad_clamp_fusion.2), kind=kCustom, calls=%fused_computation.clone | custom fusion | bytes 444096 | tf_op jit(solution)/shard_map/jit(_take)/gather | solution.py:40
  17.6 1.7 reshape.166
  20.0 2.2 broadcast_select_fusion.3
  24.0 2.2 fusion.4
  27.9 1.8 copy.63
  29.7 7.3 %all-to-all-start = ((bf16[27,8,2,256]{3,2,0,1:T(2,128)(2,1)}), bf16[27,8,2,256]{3,2,0,1:T(2,128)(2,1)}, u32[]{:S(2)}, u32[]{:S(2)}) async-start(bf16[27,8,2,256]{3,2,0,1:T(2,128)(2,1)} %copy.63), calls=%async_computation | async-start | bytes 442368 | tf_op jit(solution)/shard_map/all_to_all | solution.py:77
  44.0 1.7 reshape.143
  47.1 18.5 %gather_fusion = bf16[6912,256]{1,0:T(8,128)(2,1)} fusion(bf16[256,256]{1,0:T(8,128)(2,1)} %bitcast_select_fusion.1, s32[7168]{0:T(1024)} %pad_clamp_fusion), kind=kCustom, calls=%fused_computation.2 | custom fusion | bytes 7105536 | tf_op jit(solution)/shard_map/jit(_take)/gather | solution.py:40
  65.5 6.4 %reshape.142 = bf16[256,27,256]{2,1,0:T(8,128)(2,1)} reshape(bf16[6912,256]{1,0:T(8,128)(2,1)} %gather_fusion) | data formatting | bytes 7077888 | tf_op jit(solution)/shard_map/jit(_take)/gather | solution.py:40
  74.1 7.7 %select_select_fusion = bf16[256,27,256]{2,1,0:T(8,128)(2,1)} fusion(bf16[256,27,256]{2,1,0:T(8,128)(2,1)} %reshape.142, pred[256,27]{1,0:T(8,128)(4,1)} %copy.56, pred[256,27]{1,0:T(8,128)(4,1)} %bitcast.74), kind=kLoop, calls=%fused_computation.5 | loop fusion | flops 3538944 | bytes 7091712 | tf_op jit(solution)/shard_map/jit(_where)/select_n | solution.py:41
  81.8 7.4 %copy.66 = bf16[256,27,256]{0,2,1:T(8,128)(2,1)} copy(bf16[256,27,256]{2,1,0:T(8,128)(2,1)} %select_select_fusion) | data formatting | bytes 7077888 | tf_op jit(solution)/shard_map/jit(_where)/select_n | solution.py:41
  95.5 3.8 %fusion.7 = f32[256,256]{1,0:T(8,128)} fusion(bf16[256,27,256]{0,2,1:T(8,128)(2,1)} %copy.66, bf16[1,27,256,256]{3,2,1,0:T(8,128)(2,1)S(1)} %copy-done), kind=kOutput, calls=%fused_computation.11 | convolution fusion | flops 905969664 | bytes 7340032 | tf_op jit(solution)/shard_map/dot_general | solution.py:57
  101.3 2.1 reshape.153
  103.4 4.7 %scatter_fusion = f32[256,256]{1,0:T(8,128)} fusion(f32[256,256]{1,0:T(8,128)} %fusion.7, s32[432]{0:T(512)S(1)} %bitcast.75, f32[432,256]{1,0:T(8,128)} %reshape.153), kind=kCustom, calls=%fused_computation.3 | custom fusion | flops 110592 | bytes 1328832 | tf_op jit(solution)/shard_map/scatter-add | solution.py:87
  108.1 1.8 bitcast_select_fusion
  110.5 5.9 %fusion.10 = f32[27,256,256]{2,1,0:T(8,128)} fusion(bf16[256,27,256]{0,2,1:T(8,128)(2,1)} %copy.66, bf16[256,256]{1,0:T(8,128)(2,1)S(1)} %get-tuple-element.14), kind=kOutput, calls=%fused_computation.18 | convolution fusion | flops 905969664 | bytes 10747904 | tf_op jit(solution)/shard_map/dot_general | solution.py:60
  116.5 3.1 %gather_fusion.2 = bf16[432,256]{1,0:T(8,128)(2,1)} fusion(bf16[256,256]{1,0:T(8,128)(2,1)} %copy-done.1, s32[1024]{0:T(1024)S(1)} %pad_clamp_fusion.1), kind=kCustom, calls=%fused_computation.1.clone | custom fusion | bytes 444096 | tf_op jit(solution)/shard_map/jit(_take)/gather | solution.py:40
  123.1 2.0 collective-permute-start.1
  125.1 2.2 fusion.17
  128.8 2.4 collective-permute-start.3
  132.6 2.4 collective-permute-start.5
  144.0 7.3 %add_multiply_fusion = f32[27,256,256]{2,1,0:T(8,128)} fusion(f32[27,256,256]{2,1,0:T(8,128)} %fusion.10, bf16[27,16,256]{2,1,0:T(8,128)(2,1)} %reshape.120, bf16[27,16,256]{2,1,0:T(8,128)(2,1)} %reshape_reshape.3), kind=kOutput, calls=%fused_computation.4 | convolution fusion | flops 60162048 | bytes 14598144 | tf_op jit(solution)/shard_map/dot_general | solution.py:79
  152.6 2.3 collective-permute-done
  154.9 125.9 %reduce-scatter.2.cloned.1.call-done = f32[864,256]{1,0:T(8,128)} async-done(((f32[6912,256]{1,0:T(8,128)}), f32[864,256]{1,0:T(8,128)}) %reduce-scatter.2.cloned.1.call-update) | async-done | bytes 884752 | tf_op jit(solution)/shard_map/reduce_scatter | solution.py:91
  (73 shorter events, 49.2 us)
Async XLA Ops:
  7.2 16.8 %copy-start = (bf16[1,27,256,256]{3,2,1,0:T(8,128)(2,1)S(1)}, bf16[1,27,256,256]{3,2,1,0:T(8,128)(2,1)}, u32[]{:S(2)}) copy-start(bf16[1,27,256,256]{3,2,1,0:T(8,128)(2,1)} %param.11) | copy-start | bytes 10616836
  17.6 24.4 %copy-start.2 = (s32[1,1,27,8,2]{2,4,3,1,0:T(2,128)S(1)}, s32[1,1,27,8,2]{2,4,3,1,0:T(2,128)}, u32[]{:S(2)}) copy-start(s32[1,1,27,8,2]{2,4,3,1,0:T(2,128)} %param.15) | copy-start | bytes 5188
  29.7 69.6 %all-to-all-start = ((bf16[27,8,2,256]{3,2,0,1:T(2,128)(2,1)}), bf16[27,8,2,256]{3,2,0,1:T(2,128)(2,1)}, u32[]{:S(2)}, u32[]{:S(2)}) async-start(bf16[27,8,2,256]{3,2,0,1:T(2,128)(2,1)} %copy.63), calls=%async_computation | async-start | bytes 442368 | tf_op jit(solution)/shard_map/all_to_all | solution.py:77
  37.0 243.8 %reduce-scatter.2.cloned.1.call-start = ((), (), s32[]{:S(2)}) async-start(), calls=%async_computation.2 | async-start | bytes 7962624 | tf_op jit(solution)/shard_map/reduce_scatter | solution.py:91
  81.8 10.3 %copy-start.3 = (s32[27,8,2]{0,2,1:T(2,128)S(1)}, s32[27,8,2]{0,2,1:T(2,128)}, u32[]{:S(2)}) copy-start(s32[27,8,2]{0,2,1:T(2,128)} %get-tuple-element.4) | copy-start | bytes 5188
  81.8 12.1 %copy-start.5 = (pred[27,8,2]{0,2,1:T(4,128)(4,1)S(1)}, pred[27,8,2]{0,2,1:T(4,128)(4,1)}, u32[]{:S(2)}) copy-start(pred[27,8,2]{0,2,1:T(4,128)(4,1)} %get-tuple-element.3) | copy-start | bytes 1300
  81.8 12.9 %copy-start.4 = (pred[27,8,2]{0,2,1:T(4,128)(4,1)S(1)}, pred[27,8,2]{0,2,1:T(4,128)(4,1)}, u32[]{:S(2)}) copy-start(pred[27,8,2]{0,2,1:T(4,128)(4,1)} %compare_bitcast_fusion) | copy-start | bytes 1300
  95.5 7.9 %copy-start.6 = (s32[432,1]{0,1:T(1,128)S(1)}, s32[432,1]{0,1:T(1,128)}, u32[]{:S(2)}) copy-start(s32[432,1]{0,1:T(1,128)} %compare_select_fusion.2) | copy-start | bytes 5188
  103.4 4.7 %copy-start.7 = (pred[256]{0:T(512)(128)(4,1)S(1)}, pred[256]{0:T(512)(128)(4,1)}, u32[]{:S(2)}) copy-start(pred[256]{0:T(512)(128)(4,1)} %compare_bitcast_fusion.2) | copy-start | bytes 772
  109.9 0.7 copy-start.1
  123.1 11.9 %collective-permute-start.1 = (bf16[1,27,1,2,256]{4,3,0,1,2:T(2,128)(2,1)S(1)}, bf16[1,27,1,2,256]{4,3,0,1,2:T(2,128)(2,1)S(1)}, u32[]{:S(2)}, u32[]{:S(2)}) collective-permute-start(bf16[1,27,1,2,256]{4,3,0,1,2:T(2,128)(2,1)S(1)} %get-tuple-element.13), channel_id=1, source_target_pairs={{0,1},{1,2},{2,3},{3,4},{4,5},{5,6},{6,7},{7,0},{8,9},{9,10},{10,1... | collective-permute-start | bytes 82952 | tf_op jit(solution)/shard_map/ppermute | solution.py:28
  127.3 9.8 %collective-permute-start.2 = (bf16[1,27,1,2,256]{4,3,0,1,2:T(2,128)(2,1)S(1)}, bf16[1,27,1,2,256]{4,3,0,1,2:T(2,128)(2,1)S(1)}, u32[]{:S(2)}, u32[]{:S(2)}) collective-permute-start(bf16[1,27,1,2,256]{4,3,0,1,2:T(2,128)(2,1)S(1)} %get-tuple-element.12), channel_id=1, source_target_pairs={{0,2},{1,3},{2,4},{3,5},{4,6},{5,7},{6,0},{7,1},{8,10},{9,11},{10,... | collective-permute-start | bytes 82952 | tf_op jit(solution)/shard_map/ppermute | solution.py:28
  128.8 10.4 %collective-permute-start.3 = (bf16[1,27,1,2,256]{4,3,0,1,2:T(2,128)(2,1)S(1)}, bf16[1,27,1,2,256]{4,3,0,1,2:T(2,128)(2,1)S(1)}, u32[]{:S(2)}, u32[]{:S(2)}) collective-permute-start(bf16[1,27,1,2,256]{4,3,0,1,2:T(2,128)(2,1)S(1)} %get-tuple-element.11), channel_id=1, source_target_pairs={{0,3},{1,4},{2,5},{3,6},{4,7},{5,0},{6,1},{7,2},{8,11},{9,12},{10,... | collective-permute-start | bytes 82952 | tf_op jit(solution)/shard_map/ppermute | solution.py:28
  131.1 8.6 %collective-permute-start.4 = (bf16[1,27,1,2,256]{4,3,0,1,2:T(2,128)(2,1)S(1)}, bf16[1,27,1,2,256]{4,3,0,1,2:T(2,128)(2,1)S(1)}, u32[]{:S(2)}, u32[]{:S(2)}) collective-permute-start(bf16[1,27,1,2,256]{4,3,0,1,2:T(2,128)(2,1)S(1)} %get-tuple-element.10), channel_id=1, source_target_pairs={{0,4},{1,5},{2,6},{3,7},{4,0},{5,1},{6,2},{7,3},{8,12},{9,13},{10,... | collective-permute-start | bytes 82952 | tf_op jit(solution)/shard_map/ppermute | solution.py:28
  132.6 7.8 %collective-permute-start.5 = (bf16[1,27,1,2,256]{4,3,0,1,2:T(2,128)(2,1)S(1)}, bf16[1,27,1,2,256]{4,3,0,1,2:T(2,128)(2,1)S(1)}, u32[]{:S(2)}, u32[]{:S(2)}) collective-permute-start(bf16[1,27,1,2,256]{4,3,0,1,2:T(2,128)(2,1)S(1)} %get-tuple-element.9), channel_id=1, source_target_pairs={{0,5},{1,6},{2,7},{3,0},{4,1},{5,2},{6,3},{7,4},{8,13},{9,14},{10,... | collective-permute-start | bytes 82952 | tf_op jit(solution)/shard_map/ppermute | solution.py:28
  135.0 6.1 %collective-permute-start.6 = (bf16[1,27,1,2,256]{4,3,0,1,2:T(2,128)(2,1)S(1)}, bf16[1,27,1,2,256]{4,3,0,1,2:T(2,128)(2,1)S(1)}, u32[]{:S(2)}, u32[]{:S(2)}) collective-permute-start(bf16[1,27,1,2,256]{4,3,0,1,2:T(2,128)(2,1)S(1)} %get-tuple-element.8), channel_id=1, source_target_pairs={{0,6},{1,7},{2,0},{3,1},{4,2},{5,3},{6,4},{7,5},{8,14},{9,15},{10,... | collective-permute-start | bytes 82952 | tf_op jit(solution)/shard_map/ppermute | solution.py:28
  137.1 4.6 %collective-permute-start.7 = (bf16[1,27,1,2,256]{4,3,0,1,2:T(2,128)(2,1)S(1)}, bf16[1,27,1,2,256]{4,3,0,1,2:T(2,128)(2,1)S(1)}, u32[]{:S(2)}, u32[]{:S(2)}) collective-permute-start(bf16[1,27,1,2,256]{4,3,0,1,2:T(2,128)(2,1)S(1)} %get-tuple-element.7), channel_id=1, source_target_pairs={{0,7},{1,0},{2,1},{3,2},{4,3},{5,4},{6,5},{7,6},{8,15},{9,8},{10,9... | collective-permute-start | bytes 82952 | tf_op jit(solution)/shard_map/ppermute | solution.py:28
  151.3 3.6 %collective-permute-start = (bf16[256,256]{1,0:T(8,128)(2,1)}, bf16[256,256]{1,0:T(8,128)(2,1)}, u32[]{:S(2)}, u32[]{:S(2)}) collective-permute-start(bf16[256,256]{1,0:T(8,128)(2,1)} %get-tuple-element.15), channel_id=1, source_target_pairs={{8,0},{16,8},{24,16},{9,1},{17,9},{25,17},{10,2},{18,10},{26,18},{... | collective-permute-start | bytes 393224 | tf_op jit(solution)/shard_map/ppermute | solution.py:36
Sparse Core Ops, SparseCore 0:
  151.4 129.2 reduce-scatter.1
